TPU v7x, 32 devices: a whole 2x2x4 slice. The times are simulated.
32 devices in a mesh: fsdp: 4 (over z), ctx: 8 (over y, x, core).
Axes of the slice: x: 2, y: 2, z: 4, core: 2. Of those that a mesh axis runs over, the one named last changes fastest.
Arguments:
- hidden_in: bfloat16 [4, 1024, 1024], P('fsdp', 'ctx'), may hold values from -6 to 6
- pair_table: int32 [8, 2], replicated, may hold values from 0 to 15, as said below
- attn_gain: float32 [1024], replicated, may hold values from 0.5 to 1.5
- query_proj: bfloat16 [1024, 2048], P('fsdp'), may hold values from -0.1875 to 0.1875
- key_proj: bfloat16 [1024, 1024], P('fsdp'), may hold values from -0.1875 to 0.1875
- value_proj: bfloat16 [1024, 1024], P('fsdp'), may hold values from -0.1875 to 0.1875
- query_gain: float32 [128], replicated, may hold values from 0.6 to 5
- key_gain: float32 [128], replicated, may hold values from 0.6 to 5
- output_proj: bfloat16 [1024, 2048], P('fsdp'), may hold values from -2 to 2
- mlp_gain: float32 [1024], replicated, may hold values from 0.5 to 1.5
- gate_proj: bfloat16 [1024, 3072], P('fsdp'), may hold values from -0.1875 to 0.1875
- up_proj: bfloat16 [1024, 3072], P('fsdp'), may hold values from -0.1875 to 0.1875
- down_proj: bfloat16 [1024, 3072], P('fsdp'), may hold values from -0.109375 to 0.109375
- cotangent: bfloat16 [4, 1024, 1024], P('fsdp', 'ctx'), may hold values from -6 to 6
Outputs:
- block_out: bfloat16 [4, 1024, 1024], P('fsdp', 'ctx')
- input_grad: float32 [4, 1024, 1024], P('fsdp', 'ctx')
- attn_gain_grad: float32 [1024], replicated
- query_proj_grad: float32 [1024, 2048], P('fsdp')
- key_proj_grad: float32 [1024, 1024], P('fsdp')
- value_proj_grad: float32 [1024, 1024], P('fsdp')
- query_gain_grad: float32 [128], replicated
- key_gain_grad: float32 [128], replicated
- output_proj_grad: float32 [1024, 2048], P('fsdp')
- mlp_gain_grad: float32 [1024], replicated
- gate_proj_grad: float32 [1024, 3072], P('fsdp')
- up_proj_grad: float32 [1024, 3072], P('fsdp')
- down_proj_grad: float32 [1024, 3072], P('fsdp')
Inputs may be any that keep to these rules, and one draw needn't show every extreme that they name: `pair_table`: row c is (p, 15 - p); the p of the rows are 0 to 7, each once.
All inputs are finite; a program needn't handle non-finite values.
Results may differ from a plain program's by a relative error of at most 0.028.
The roundings to bfloat16 on the way count: a program that leaves them out, or rounds other values in their place, can miss the bound.
Values may be sent and summed in bfloat16 or wider, within the bound.
No kernel may reach another device: no remote copies, remote signals or barrier semaphores. Data moves between devices by JAX's collectives and lax.ppermute only.
A program may use at most 320 MiB of HBM per device.

v0:
```python
import math
import jax
import jax.numpy as jnp
from jax import lax
from jax.sharding import PartitionSpec as P

NORM_EPS = 1e-06
ROPE_BASE = 1000000.0
MASKED = -1e30


def rms_norm(values, gain_vec):
    return (
        values * lax.rsqrt(jnp.mean(values * values, axis=-1, keepdims=True) + NORM_EPS) * gain_vec
    )


def rotate(values, angles):
    half_width = values.shape[-1] // 2
    cosine = jnp.cos(angles)[:, None, :]
    sine_part = jnp.sin(angles)[:, None, :]
    first_half = values[..., :half_width]
    second_half = values[..., half_width:]
    return jnp.concatenate(
        [
            first_half * cosine - second_half * sine_part,
            second_half * cosine + first_half * sine_part,
        ],
        axis=-1,
    )


def head_prep(raw_heads, gain_vec, angles):
    return rotate(rms_norm(raw_heads, gain_vec), angles)


def angle_table(positions, head_width):
    half_width = head_width // 2
    frequency = ROPE_BASE ** (-(jnp.arange(half_width, dtype=jnp.float32) * 2.0 / head_width))
    return positions.astype(jnp.float32)[:, None] * frequency[None, :]


def token_positions(pair_table, row_count, block_len):
    index_rows = jnp.arange(row_count, dtype=jnp.int32)
    owners = index_rows // (2 * block_len)
    halves = index_rows // block_len % 2
    return pair_table[owners, halves] * block_len + index_rows % block_len


def times_transposed(lhs_mat, rhs_mat):
    return lax.dot_general(
        lhs_mat, rhs_mat, (((1,), (1,)), ((), ())), preferred_element_type=jnp.float32
    )


def transposed_times(lhs_mat, rhs_mat):
    return lax.dot_general(
        lhs_mat, rhs_mat, (((0,), (0,)), ((), ())), preferred_element_type=jnp.float32
    )


def block_scores(grouped_query, key_blk, query_pos, key_pos_blk, score_scale):
    raw_scores = (
        jnp.einsum("qhgd,khd->hgqk", grouped_query, key_blk, preferred_element_type=jnp.float32)
        * score_scale
    )
    allowed = key_pos_blk[None, :] <= query_pos[:, None]
    return (jnp.where(allowed[None, None], raw_scores, MASKED), allowed)


def on_device(
    hidden_in,
    pair_table,
    attn_gain,
    query_proj,
    key_proj,
    value_proj,
    query_gain,
    key_gain,
    output_proj,
    mlp_gain,
    gate_proj,
    up_proj,
    down_proj,
    cotangent,
):
    query_w, key_w, value_w, output_w = (
        lax.all_gather(query_proj, "fsdp", axis=0, tiled=True),
        lax.all_gather(key_proj, "fsdp", axis=0, tiled=True),
        lax.all_gather(value_proj, "fsdp", axis=0, tiled=True),
        lax.all_gather(output_proj, "fsdp", axis=0, tiled=True),
    )
    gate_w, upper_w, down_w = (
        lax.all_gather(gate_proj, "fsdp", axis=0, tiled=True),
        lax.all_gather(up_proj, "fsdp", axis=0, tiled=True),
        lax.all_gather(down_proj, "fsdp", axis=0, tiled=True),
    )
    inputs = hidden_in[0]
    cot_low = cotangent[0]
    row_count = inputs.shape[0]
    block_len = row_count // 2
    ctx_count = lax.axis_size("ctx")
    ctx_index = lax.axis_index("ctx")
    head_width = query_gain.shape[0]
    query_count = query_w.shape[1] // head_width
    kvhead_count = key_w.shape[1] // head_width
    group_size = query_count // kvhead_count
    score_scale = 1.0 / math.sqrt(head_width)
    local_rows = jnp.arange(block_len, dtype=jnp.int32)
    own_pos = jnp.concatenate(
        [
            pair_table[ctx_index, 0] * block_len + local_rows,
            pair_table[ctx_index, 1] * block_len + local_rows,
        ]
    )
    total_keys = ctx_count * row_count
    key_pos = token_positions(pair_table, total_keys, block_len)
    key_block = math.gcd(total_keys, 512)
    block_count = total_keys // key_block
    angles = angle_table(own_pos, head_width)

    def head_query(raw_heads, gain_vec):
        return head_prep(raw_heads, gain_vec, angles)

    input_wide = inputs.astype(jnp.float32)
    attn_in = rms_norm(input_wide, attn_gain).astype(jnp.bfloat16)
    query_raw = jnp.dot(attn_in, query_w, preferred_element_type=jnp.float32).reshape(
        row_count, query_count, head_width
    )
    key_raw = jnp.dot(attn_in, key_w, preferred_element_type=jnp.float32).reshape(
        row_count, kvhead_count, head_width
    )
    value_raw = jnp.dot(attn_in, value_w, preferred_element_type=jnp.float32)
    query_heads = head_query(query_raw, query_gain).astype(jnp.bfloat16)
    key_heads = head_query(key_raw, key_gain).astype(jnp.bfloat16)
    value_heads = value_raw.astype(jnp.bfloat16)
    key_all, value_all = (
        lax.all_gather(key_heads.reshape(row_count, -1), "ctx", axis=0, tiled=True),
        lax.all_gather(value_heads, "ctx", axis=0, tiled=True),
    )
    key_blocks = key_all.reshape(block_count, key_block, kvhead_count, head_width)
    value_blocks = value_all.reshape(block_count, key_block, kvhead_count, head_width)
    pos_blocks = key_pos.reshape(block_count, key_block)
    grouped_query = query_heads.reshape(row_count, kvhead_count, group_size, head_width)

    def stats_step(state_pair, block_data):
        running_max, running_sum = state_pair
        key_blk, pos_blk = block_data
        scores, allowed = block_scores(grouped_query, key_blk, own_pos, pos_blk, score_scale)
        new_max = jnp.maximum(running_max, jnp.max(scores, axis=-1))
        weights_now = jnp.where(allowed[None, None], jnp.exp(scores - new_max[..., None]), 0.0)
        running_sum = running_sum * jnp.exp(running_max - new_max) + jnp.sum(weights_now, axis=-1)
        return ((new_max, running_sum), None)

    stat_shape = (kvhead_count, group_size, row_count)
    (row_max, row_sum), unused = lax.scan(
        stats_step,
        (jnp.full(stat_shape, MASKED, jnp.float32), jnp.zeros(stat_shape, jnp.float32)),
        (key_blocks, pos_blocks),
    )
    log_total = row_max + jnp.log(row_sum)

    def mix_step(accum, block_data):
        key_blk, value_blk, pos_blk = block_data
        scores, allowed = block_scores(grouped_query, key_blk, own_pos, pos_blk, score_scale)
        probs = jnp.exp(scores - log_total[..., None]).astype(jnp.bfloat16)
        return (
            accum
            + jnp.einsum("hgqk,khd->qhgd", probs, value_blk, preferred_element_type=jnp.float32),
            None,
        )

    mixed, unused = lax.scan(
        mix_step,
        jnp.zeros((row_count, kvhead_count, group_size, head_width), jnp.float32),
        (key_blocks, value_blocks, pos_blocks),
    )
    attn_mix = mixed.reshape(row_count, -1).astype(jnp.bfloat16)
    resid = input_wide + times_transposed(attn_mix, output_w)
    mlp_in = rms_norm(resid, mlp_gain).astype(jnp.bfloat16)
    gate = jnp.dot(mlp_in, gate_w, preferred_element_type=jnp.float32)
    upper = jnp.dot(mlp_in, upper_w, preferred_element_type=jnp.float32)
    sigma = jax.nn.sigmoid(gate)
    hidden_act = (gate * sigma * upper).astype(jnp.bfloat16)
    block_out = (resid + times_transposed(hidden_act, down_w)).astype(jnp.bfloat16)
    hidden_grad = jnp.dot(cot_low, down_w, preferred_element_type=jnp.float32)
    gate_low = (hidden_grad * upper * sigma * (1.0 + gate * (1.0 - sigma))).astype(jnp.bfloat16)
    upper_low = (hidden_grad * gate * sigma).astype(jnp.bfloat16)
    mlp_in_grad = times_transposed(gate_low, gate_w) + times_transposed(upper_low, upper_w)
    resid_part, mlp_gain_grad = jax.vjp(rms_norm, resid, mlp_gain)[1](mlp_in_grad)
    resid_grad = cot_low.astype(jnp.float32) + resid_part
    resid_low = resid_grad.astype(jnp.bfloat16)
    mix_grad = jnp.dot(resid_low, output_w, preferred_element_type=jnp.float32).astype(jnp.bfloat16)
    dmix_heads = mix_grad.reshape(row_count, kvhead_count, group_size, head_width)
    delta = jnp.einsum(
        "qhgd,qhgd->hgq",
        dmix_heads,
        attn_mix.reshape(row_count, kvhead_count, group_size, head_width),
        preferred_element_type=jnp.float32,
    )

    def grad_step(query_accum, block_data):
        key_blk, value_blk, pos_blk = block_data
        scores, allowed = block_scores(grouped_query, key_blk, own_pos, pos_blk, score_scale)
        probs = jnp.exp(scores - log_total[..., None])
        value_part = jnp.einsum(
            "hgqk,qhgd->khd",
            probs.astype(jnp.bfloat16),
            dmix_heads,
            preferred_element_type=jnp.float32,
        )
        prob_grad = jnp.einsum(
            "qhgd,khd->hgqk", dmix_heads, value_blk, preferred_element_type=jnp.float32
        )
        score_grad = (probs * (prob_grad - delta[..., None]) * score_scale).astype(jnp.bfloat16)
        query_accum = query_accum + jnp.einsum(
            "hgqk,khd->qhgd", score_grad, key_blk, preferred_element_type=jnp.float32
        )
        key_part = jnp.einsum(
            "hgqk,qhgd->khd", score_grad, grouped_query, preferred_element_type=jnp.float32
        )
        return (query_accum, (key_part, value_part))

    query_grad, (key_parts, value_parts) = lax.scan(
        grad_step,
        jnp.zeros((row_count, kvhead_count, group_size, head_width), jnp.float32),
        (key_blocks, value_blocks, pos_blocks),
    )
    key_grad, value_grad = (
        lax.psum_scatter(
            key_parts.reshape(total_keys, -1).astype(jnp.bfloat16),
            "ctx",
            scatter_dimension=0,
            tiled=True,
        ).astype(jnp.float32),
        lax.psum_scatter(
            value_parts.reshape(total_keys, -1).astype(jnp.bfloat16),
            "ctx",
            scatter_dimension=0,
            tiled=True,
        ).astype(jnp.float32),
    )
    query_raw_grad, query_gain_grad = jax.vjp(head_query, query_raw, query_gain)[1](
        query_grad.reshape(row_count, query_count, head_width)
    )
    key_raw_grad, key_gain_grad = jax.vjp(head_query, key_raw, key_gain)[1](
        key_grad.reshape(row_count, kvhead_count, head_width)
    )
    query_low = query_raw_grad.reshape(row_count, -1).astype(jnp.bfloat16)
    key_low = key_raw_grad.reshape(row_count, -1).astype(jnp.bfloat16)
    value_low = value_grad.astype(jnp.bfloat16)
    attn_in_grad = (
        times_transposed(query_low, query_w)
        + times_transposed(key_low, key_w)
        + times_transposed(value_low, value_w)
    )
    input_part, attn_gain_grad = jax.vjp(rms_norm, input_wide, attn_gain)[1](attn_in_grad)
    input_grad = resid_grad + input_part
    attn_right = jnp.concatenate([query_low, key_low, value_low], axis=1)
    mlp_right = jnp.concatenate([gate_low, upper_low], axis=1)
    pairings = (
        (attn_in, attn_right),
        (resid_low, attn_mix),
        (mlp_in, mlp_right),
        (cot_low, hidden_act),
    )
    pieces = [transposed_times(operand, partner) for operand, partner in pairings]
    owned_term = lax.psum_scatter(
        jnp.concatenate(pieces, axis=1).astype(jnp.bfloat16),
        "fsdp",
        scatter_dimension=0,
        tiled=True,
    )
    owned = lax.psum(owned_term, "ctx").astype(jnp.float32)
    attn_gain_grad, query_gain_grad, key_gain_grad, mlp_gain_grad = lax.psum(
        (attn_gain_grad, query_gain_grad, key_gain_grad, mlp_gain_grad), ("fsdp", "ctx")
    )
    widths = (
        query_w.shape[1],
        key_w.shape[1],
        value_w.shape[1],
        output_w.shape[1],
        gate_w.shape[1],
        upper_w.shape[1],
        down_w.shape[1],
    )
    offsets = [0]
    for column_count in widths:
        offsets.append(offsets[-1] + column_count)
    grads = [owned[:, offsets[number] : offsets[number + 1]] for number in range(len(widths))]
    return (
        block_out[None],
        input_grad[None],
        attn_gain_grad,
        grads[0],
        grads[1],
        grads[2],
        query_gain_grad,
        key_gain_grad,
        grads[3],
        mlp_gain_grad,
        grads[4],
        grads[5],
        grads[6],
    )


def solution(mesh):
    in_specs = (
        P("fsdp", "ctx", None),
        P(),
        P(),
        P("fsdp", None),
        P("fsdp", None),
        P("fsdp", None),
        P(),
        P(),
        P("fsdp", None),
        P(),
        P("fsdp", None),
        P("fsdp", None),
        P("fsdp", None),
        P("fsdp", "ctx", None),
    )
    out_specs = (
        P("fsdp", "ctx", None),
        P("fsdp", "ctx", None),
        P(),
        P("fsdp", None),
        P("fsdp", None),
        P("fsdp", None),
        P(),
        P(),
        P("fsdp", None),
        P(),
        P("fsdp", None),
        P("fsdp", None),
        P("fsdp", None),
    )
    return jax.shard_map(
        on_device, mesh=mesh, in_specs=in_specs, out_specs=out_specs, check_vma=False
    )
```

profile of v0, /device:TPU:0, one launch (start us, length us, event | category | flops | bytes accessed | tf_op | source)
XLA Modules:
  0.0 1498.1 jit_solution(4632809275431126359)
XLA Ops:
  10.6 47.4 %all-gather.10.cloned.1.call-done = bf16[1024,1024]{1,0:T(8,128)(2,1)} async-done(((bf16[256,1024]{1,0:T(8,128)(2,1)}), bf16[1024,1024]{1,0:T(8,128)(2,1)}) %all-gather.10.cloned.1.call-update) | async-done | bytes 2097168 | tf_op jit(solution)/shard_map/all_gather | solution.py:90
  63.2 40.9 %all-gather.14.cloned.1.call-done = bf16[1024,1024]{1,0:T(8,128)(2,1)} async-done(((bf16[256,1024]{1,0:T(8,128)(2,1)}), bf16[1024,1024]{1,0:T(8,128)(2,1)}) %all-gather.14.cloned.1.call-update) | async-done | bytes 2097168 | tf_op jit(solution)/shard_map/all_gather | solution.py:89
  114.5 8.8 gather_fusion
  123.4 61.8 %all-gather.18.cloned.1.call-done = bf16[1024,2048]{1,0:T(8,128)(2,1)} async-done(((bf16[256,2048]{1,0:T(8,128)(2,1)}), bf16[1024,2048]{1,0:T(8,128)(2,1)}) %all-gather.18.cloned.1.call-update) | async-done | bytes 4194320 | tf_op jit(solution)/shard_map/all_gather | solution.py:88
  185.2 6.4 copy.62
  197.6 16.2 %all-gather.12.cloned.1.call-done = bf16[1024,1024]{1,0:T(8,128)(2,1)} async-done(((bf16[128,1024]{1,0:T(8,128)(2,1)}), bf16[1024,1024]{1,0:T(8,128)(2,1)}) %all-gather.12.cloned.1.call-update) | async-done | bytes 2097168 | tf_op jit(solution)/shard_map/all_gather | solution.py:139
  217.4 26.6 %all-gather.16.cloned.1.call-done = bf16[1024,1024]{1,0:T(8,128)(2,1)} async-done(((bf16[128,1024]{1,0:T(8,128)(2,1)}), bf16[1024,1024]{1,0:T(8,128)(2,1)}) %all-gather.16.cloned.1.call-update) | async-done | bytes 2097168 | tf_op jit(solution)/shard_map/all_gather | solution.py:138
  250.6 17.8 %while.40 = (s32[]{:T(128)}, f32[128,8,2,128]{0,3,2,1:T(8,128)}, bf16[2,512,8,128]{3,2,1,0:T(8,128)(2,1)}, s32[2,512]{1,0:T(2,128)S(1)}, s32[128]{0:T(128)S(1)},...) while((s32[]{:T(128)}, f32[128,8,2,128]{0,3,2,1:T(8,128)}, ...), condition=%wide.region_8.9_spmd.clone, body=%wide.region_7.8_spmd.clone.sunk | while | flops 541655040 | bytes 9058947 | solution.py:173
  270.5 55.6 %all-gather.20.cloned.1.call-done = bf16[1024,2048]{1,0:T(8,128)(2,1)} async-done(((bf16[256,2048]{1,0:T(8,128)(2,1)}), bf16[1024,2048]{1,0:T(8,128)(2,1)}) %all-gather.20.cloned.1.call-update) | async-done | bytes 4194320 | tf_op jit(solution)/shard_map/all_gather | solution.py:91
  330.9 110.6 %all-gather.24.cloned.1.call-done = bf16[1024,3072]{1,0:T(8,128)(2,1)} async-done(((bf16[256,3072]{1,0:T(8,128)(2,1)}), bf16[1024,3072]{1,0:T(8,128)(2,1)}) %all-gather.24.cloned.1.call-update) | async-done | bytes 6291472 | tf_op jit(solution)/shard_map/all_gather | solution.py:95
  446.6 110.1 %all-gather.22.cloned.1.call-done = bf16[1024,3072]{1,0:T(8,128)(2,1)} async-done(((bf16[256,3072]{1,0:T(8,128)(2,1)}), bf16[1024,3072]{1,0:T(8,128)(2,1)}) %all-gather.22.cloned.1.call-update) | async-done | bytes 6291472 | tf_op jit(solution)/shard_map/all_gather | solution.py:94
  561.7 110.1 %all-gather.26.cloned.1.call-done = bf16[1024,3072]{1,0:T(8,128)(2,1)} async-done(((bf16[256,3072]{1,0:T(8,128)(2,1)}), bf16[1024,3072]{1,0:T(8,128)(2,1)}) %all-gather.26.cloned.1.call-update) | async-done | bytes 6291472 | tf_op jit(solution)/shard_map/all_gather | solution.py:96
  671.8 6.5 multiply_convert_fusion
  680.6 5.3 multiply_reduce_fusion.4
  698.9 19.8 %while.41 = (s32[]{:T(128)}, f32[128,8,2,128]{0,3,2,1:T(8,128)}, bf16[2,512,8,128]{3,1,2,0:T(8,128)(2,1)}, bf16[2,512,8,128]{3,1,2,0:T(8,128)(2,1)}, bf16[2,512,...) while((s32[]{:T(128)}, f32[128,8,2,128]{0,3,2,1:T(8,128)}, ...), condition=%wide.region_12.13_spmd.clone, body=%wide.region_11.12_spmd.clone.sunk | while | flops 1354301440 | bytes 76774256 | solution.py:224
  740.2 6.6 convolution_convert_fusion
  746.8 16.2 %reduce-scatter.6.cloned.1.call-done = bf16[128,1024]{1,0:T(8,128)(2,1)} async-done(((bf16[1024,1024]{1,0:T(8,128)(2,1)}), bf16[128,1024]{1,0:T(8,128)(2,1)}) %reduce-scatter.6.cloned.1.call-update) | async-done | bytes 262160 | tf_op jit(solution)/shard_map/reduce_scatter | solution.py:230
  765.3 42.7 %reduce-scatter.8.cloned.1.call-done = bf16[128,1024]{1,0:T(8,128)(2,1)} async-done(((bf16[1024,1024]{1,0:T(8,128)(2,1)}), bf16[128,1024]{1,0:T(8,128)(2,1)}) %reduce-scatter.8.cloned.1.call-update) | async-done | bytes 262160 | tf_op jit(solution)/shard_map/reduce_scatter | solution.py:236
  809.2 7.1 convolution_convert_fusion.1
  816.3 19.7 %pad_maximum_fusion = bf16[1024,15360]{1,0:T(8,128)(2,1)} fusion(bf16[1024,3072]{1,0:T(8,128)(2,1)S(1)} %bitcast.290, bf16[1024,6144]{1,0:T(8,128)(2,1)} %convolution_convert_fusion, bf16[1024,2048]{1,0:T(8,128)(2,1)} %convolution_convert_fusion.2, bf16[1024,4096]{1,0:T(8,128)(2,1)} %convolution_convert_fusion.1), kind=kLoop, calls=%fused_computation.60 | loop fusion | flops 125829120 | bytes 62914560 | tf_op jit(solution)/shard_map/concatenate | solution.py:269
  836.3 515.3 %reduce-scatter.10.cloned.1.call-done = bf16[256,15360]{1,0:T(8,128)(2,1)} async-done(((bf16[1024,15360]{1,0:T(8,128)(2,1)}), bf16[256,15360]{1,0:T(8,128)(2,1)}) %reduce-scatter.10.cloned.1.call-update) | async-done | bytes 7864336
  1351.7 5.8 fusion.51
  1361.5 43.2 %all-reduce.5 = (f32[1024]{0:T(1024)}, f32[128]{0:T(128)}, f32[128]{0:T(128)}, f32[1024]{0:T(1024)}) all-reduce(f32[1024]{0:T(1024)S(1)} %get-tuple-element.333, f32[128]{0:T(128)S(1)} %get-tuple-element.327, f32[128]{0:T(128)S(1)} %get-tuple-element.331, ...), channel_id=1, replica_groups=mesh['fsdp'=4,'ctx'=8] {'fsdp','ctx'}, use_global_device_ids=true, to_apply=%region_19.20 | all-reduce | flops 2304 | bytes 18432 | tf_op jit(solution)/shard_map/psum | solution.py:275
  1405.7 73.3 %all-reduce.8.cloned.1.call-done = bf16[256,15360]{1,0:T(8,128)(2,1)} async-done(((bf16[256,15360]{1,0:T(8,128)(2,1)}), bf16[256,15360]{1,0:T(8,128)(2,1)}) %all-reduce.8.cloned.1.call-update) | async-done | bytes 7864336 | tf_op jit(solution)/shard_map/psum | solution.py:274
  (245 shorter events, 148.5 us)
Async XLA Ops:
  7.2 53.8 %copy-start = (s32[8,2]{0,1:T(2,128)S(1)}, s32[8,2]{0,1:T(2,128)}, u32[]{:S(2)}) copy-start(s32[8,2]{0,1:T(2,128)} %param.21) | copy-start | bytes 196
  7.2 50.8 %all-gather.10.cloned.1.call-start = ((), (), s32[]{:S(2)}) async-start(), calls=%async_computation.3 | async-start | bytes 2621440 | tf_op jit(solution)/shard_map/all_gather | solution.py:90
  7.9 96.1 %all-gather.14.cloned.1.call-start = ((), (), s32[]{:S(2)}) async-start(), calls=%async_computation.5 | async-start | bytes 2621440 | tf_op jit(solution)/shard_map/all_gather | solution.py:89
  8.7 99.3 %copy-start.6 = (bf16[1,128,1024]{2,1,0:T(8,128)(2,1)S(1)}, bf16[1,128,1024]{2,1,0:T(8,128)(2,1)}, u32[]{:S(2)}) copy-start(bf16[1,128,1024]{2,1,0:T(8,128)(2,1)} %param.20) | copy-start | bytes 786436
  8.7 99.3 %copy-start.36 = (f32[1024]{0:T(1024)S(1)}, f32[1024]{0:T(1024)}, u32[]{:S(2)}) copy-start(f32[1024]{0:T(1024)} %param.22) | copy-start | bytes 12292
  8.7 176.5 %all-gather.18.cloned.1.call-start = ((), (), s32[]{:S(2)}) async-start(), calls=%async_computation.7 | async-start | bytes 5242880 | tf_op jit(solution)/shard_map/all_gather | solution.py:88
  9.4 204.4 %all-gather.12.cloned.1.call-start = ((), (), s32[]{:S(2)}) async-start(), calls=%async_computation.4 | async-start | bytes 2359296 | tf_op jit(solution)/shard_map/all_gather | solution.py:139
  10.6 52.3 %copy-start.40 = (f32[128]{0:T(128)}, f32[128]{0:T(128)S(1)}, u32[]{:S(2)}) copy-start(f32[128]{0:T(128)S(1)} %fusion.66) | copy-start | bytes 1540
  60.9 49.5 %copy-start.38 = (f32[128]{0:T(128)S(1)}, f32[128]{0:T(128)}, u32[]{:S(2)}) copy-start(f32[128]{0:T(128)} %param.27) | copy-start | bytes 1540
  60.9 183.0 %all-gather.16.cloned.1.call-start = ((), (), s32[]{:S(2)}) async-start(), calls=%async_computation.6 | async-start | bytes 2359296 | tf_op jit(solution)/shard_map/all_gather | solution.py:138
  111.5 214.6 %all-gather.20.cloned.1.call-start = ((), (), s32[]{:S(2)}) async-start(), calls=%async_computation.8 | async-start | bytes 5242880 | tf_op jit(solution)/shard_map/all_gather | solution.py:91
  112.1 329.5 %all-gather.24.cloned.1.call-start = ((), (), s32[]{:S(2)}) async-start(), calls=%async_computation.10 | async-start | bytes 7864320 | tf_op jit(solution)/shard_map/all_gather | solution.py:95
  112.8 443.8 %all-gather.22.cloned.1.call-start = ((), (), s32[]{:S(2)}) async-start(), calls=%async_computation.9 | async-start | bytes 7864320 | tf_op jit(solution)/shard_map/all_gather | solution.py:94
  113.6 558.2 %all-gather.26.cloned.1.call-start = ((), (), s32[]{:S(2)}) async-start(), calls=%async_computation.11 | async-start | bytes 7864320 | tf_op jit(solution)/shard_map/all_gather | solution.py:96
  114.3 648.7 %reduce-scatter.6.cloned.1.call-start = ((), (), s32[]{:S(2)}) async-start(), calls=%async_computation.12 | async-start | bytes 2359296 | tf_op jit(solution)/shard_map/reduce_scatter | solution.py:230
  268.4 61.7 %copy-start.37 = (f32[1024]{0:T(1024)S(1)}, f32[1024]{0:T(1024)}, u32[]{:S(2)}) copy-start(f32[1024]{0:T(1024)} %param.29) | copy-start | bytes 12292
  678.3 7.5 copy-start.22
  678.3 7.5 copy-start.24
  723.6 84.5 %reduce-scatter.8.cloned.1.call-start = ((), (), s32[]{:S(2)}) async-start(), calls=%async_computation.13 | async-start | bytes 2359296 | tf_op jit(solution)/shard_map/reduce_scatter | solution.py:236
  728.1 623.5 %reduce-scatter.10.cloned.1.call-start = ((), (), s32[]{:S(2)}) async-start(), calls=%async_computation.15 | async-start | bytes 39321600
  740.2 24.0 %copy-start.14 = (f32[128,8,128]{0,2,1:T(8,128)S(1)}, f32[128,8,128]{0,2,1:T(8,128)}, u32[]{:S(2)}) copy-start(f32[128,8,128]{0,2,1:T(8,128)} %copy-done.13) | copy-start | bytes 1572868
  836.0 515.6 %copy-start.19 = (bf16[128,3072]{1,0:T(8,128)(2,1)S(1)}, bf16[128,3072]{1,0:T(8,128)(2,1)}, u32[]{:S(2)}) copy-start(bf16[128,3072]{1,0:T(8,128)(2,1)} %get-tuple-element.406) | copy-start | bytes 2359300
  836.0 643.1 %all-reduce.8.cloned.1.call-start = ((), (), s32[]{:S(2)}) async-start(), calls=%async_computation.14 | async-start | bytes 15728640 | tf_op jit(solution)/shard_map/psum | solution.py:274
  1358.4 46.4 %copy-start.41 = (f32[128]{0:T(128)S(1)}, f32[128]{0:T(128)}, u32[]{:S(2)}) copy-start(f32[128]{0:T(128)} %copy-done.40) | copy-start | bytes 1540
  (40 other events, 149.0 us)
Sparse Core Ops, SparseCore 0:
  9.6 48.3 all-gather.9
  59.5 44.4 all-gather.13
  105.6 79.5 all-gather.17
  187.5 26.2 all-gather.11
  216.1 27.7 all-gather.15
  245.4 80.7 all-gather.19
  327.7 113.8 all-gather.23
  443.1 113.5 all-gather.21
  558.2 113.5 all-gather.25
  723.7 39.2 reduce-scatter.5
  766.9 41.0 reduce-scatter.7
  836.1 515.4 reduce-scatter.9
  1354.9 124.0 all-reduce.7
where the time goes:
time: 1510 us; the launch traced here: 1500 us
  waiting for transfers between devices  1230 us (81%)
  matrix products  88.8 us (6%)
  local copies, waits for them, and re-layouts  76.9 us (5%)
  blocking collectives  43.2 us (3%)
  other arithmetic  39.3 us (3%)
  between operations  16.1 us (1%)
    unnamed x14, waiting for transfers between devices  520 us
    all_gather x1, waiting for transfers between devices, on_device(): lax.all_gather(up_proj, 'fsdp', axis=0, tiled=True)  111 us
    all_gather x1, waiting for transfers between devices, on_device(): lax.all_gather(down_proj, 'fsdp', axis=0, tiled=True)  110 us
    all_gather x1, waiting for transfers between devices, on_device(): lax.all_gather(gate_proj, 'fsdp', axis=0, tiled=True)  110 us
    psum x1, waiting for transfers between devices, on_device(): owned = lax.psum(owned_term, 'ctx').astype(jnp.float32)  73.3 us
    all_gather x1, waiting for transfers between devices, on_device(): lax.all_gather(query_proj, 'fsdp', axis=0, tiled=True)  61.8 us
    all_gather x1, waiting for transfers between devices, on_device(): lax.all_gather(output_proj, 'fsdp', axis=0, tiled=True)  55.6 us
    all_gather x1, waiting for transfers between devices, on_device(): lax.all_gather(value_proj, 'fsdp', axis=0, tiled=True)  47.4 us
  transfers between devices with their start and end apart: 13, of which 13 were waited for; matrix products, arithmetic and copies ran while one was open for 7% of the time, Pallas kernels for 0%

commit v1 on v0

--- a/solution.py
+++ b/solution.py
@@ -7,6 +7,18 @@
 NORM_EPS = 1e-06
 ROPE_BASE = 1000000.0
 MASKED = -1e30
+
+
+def gather_by_bits(x, axis, dim):
+    ways, here = (lax.axis_size(axis), lax.axis_index(axis))
+    grown, reach = (x, 1)
+    while reach < ways:
+        theirs = lax.ppermute(grown, axis, [(d, d ^ reach) for d in range(ways)])
+        mine_first = jnp.concatenate([grown, theirs], axis=dim)
+        theirs_first = jnp.concatenate([theirs, grown], axis=dim)
+        grown = jnp.where(here & reach == 0, mine_first, theirs_first)
+        reach = 2 * reach
+    return grown
 
 
 def rms_norm(values, gain_vec):
@@ -92,7 +104,7 @@
     )
     gate_w, upper_w, down_w = (
         lax.all_gather(gate_proj, "fsdp", axis=0, tiled=True),
-        lax.all_gather(up_proj, "fsdp", axis=0, tiled=True),
+        gather_by_bits(up_proj, "fsdp", 0),
         lax.all_gather(down_proj, "fsdp", axis=0, tiled=True),
     )
     inputs = hidden_in[0]

time: 1510 us -> 1480 us (0.980)
  waiting for transfers between devices: 1230 us -> 1200 us
    all_gather x1 -> x0, waiting for transfers between devices: 111 us -> none  [on_device(): lax.all_gather(up_proj, 'fsdp', axis=0, tiled=True)]
    ppermute x0 -> x2, waiting for transfers between devices: none -> 93.5 us  [gather_by_bits(): theirs = lax.ppermute(grown, axis, [(d, d ^ reach) for d in range(ways)])]
    all_gather x1, waiting for transfers between devices: 61.8 us -> 0.01 us  [on_device(): lax.all_gather(query_proj, 'fsdp', axis=0, tiled=True)]
    all_gather x1, waiting for transfers between devices: 55.6 us -> 89.7 us  [on_device(): lax.all_gather(output_proj, 'fsdp', axis=0, tiled=True)]
    all_gather x1, waiting for transfers between devices: 110 us -> 130 us  [on_device(): lax.all_gather(down_proj, 'fsdp', axis=0, tiled=True)]
    unnamed x14 -> x13, waiting for transfers between devices: 520 us -> 519 us
  transfers between devices with their start and end apart: 13 -> 14, of which waited for: 13 -> 12; matrix products, arithmetic and copies ran while one was open for 7% -> 8% of each run, Pallas kernels for 0% -> 0%
where the time goes in v1:
time: 1480 us; the launch traced here: 1470 us
  waiting for transfers between devices  1200 us (81%)
  matrix products  90.7 us (6%)
  local copies, waits for them, and re-layouts  77.1 us (5%)
  blocking collectives  43.2 us (3%)
  other arithmetic  41.8 us (3%)
  between operations  16.5 us (1%)
    unnamed x13, waiting for transfers between devices  519 us
    all_gather x1, waiting for transfers between devices, on_device(): lax.all_gather(down_proj, 'fsdp', axis=0, tiled=True)  130 us
    all_gather x1, waiting for transfers between devices, on_device(): lax.all_gather(gate_proj, 'fsdp', axis=0, tiled=True)  110 us
    ppermute x2, waiting for transfers between devices, gather_by_bits(): theirs = lax.ppermute(grown, axis, [(d, d ^ reach) for d in range(ways)])  93.5 us
    all_gather x1, waiting for transfers between devices, on_device(): lax.all_gather(output_proj, 'fsdp', axis=0, tiled=True)  89.7 us
    psum x1, waiting for transfers between devices, on_device(): owned = lax.psum(owned_term, 'ctx').astype(jnp.float32)  73.2 us
    all_gather x1, waiting for transfers between devices, on_device(): lax.all_gather(value_proj, 'fsdp', axis=0, tiled=True)  47.4 us
    psum x1, blocking collectives, on_device(): lax.psum((attn_gain_grad, query_gain_grad, key_gain_grad, mlp_gain_grad),...  43.2 us
  transfers between devices with their start and end apart: 14, of which 12 were waited for; matrix products, arithmetic and copies ran while one was open for 8% of the time, Pallas kernels for 0%

profile of v1, /device:TPU:0, one launch (start us, length us, event | category | flops | bytes accessed | tf_op | source)
XLA Modules:
  0.0 1474.8 jit_solution(10687016288496532972)
XLA Ops:
  10.6 47.4 %all-gather.9.cloned.1.call-done = bf16[1024,1024]{1,0:T(8,128)(2,1)} async-done(((bf16[256,1024]{1,0:T(8,128)(2,1)}), bf16[1024,1024]{1,0:T(8,128)(2,1)}) %all-gather.9.cloned.1.call-update) | async-done | bytes 2097168 | tf_op jit(solution)/shard_map/all_gather | solution.py:102
  63.2 40.9 %all-gather.13.cloned.1.call-done = bf16[1024,1024]{1,0:T(8,128)(2,1)} async-done(((bf16[256,1024]{1,0:T(8,128)(2,1)}), bf16[1024,1024]{1,0:T(8,128)(2,1)}) %all-gather.13.cloned.1.call-update) | async-done | bytes 2097168 | tf_op jit(solution)/shard_map/all_gather | solution.py:101
  114.2 8.8 gather_fusion
  123.1 93.5 %collective-permute-done = bf16[256,3072]{1,0:T(8,128)(2,1)} collective-permute-done((bf16[256,3072]{1,0:T(8,128)(2,1)}, bf16[256,3072]{1,0:T(8,128)(2,1)}, u32[]{:S(2)}, u32[]{:S(2)}) %collective-permute-start) | collective-permute-done | bytes 1572896 | tf_op jit(solution)/shard_map/ppermute | solution.py:16
  220.2 6.4 copy.62
  232.5 13.6 all-gather.11.cloned.1.call-done
  249.6 26.6 %all-gather.15.cloned.1.call-done = bf16[1024,1024]{1,0:T(8,128)(2,1)} async-done(((bf16[128,1024]{1,0:T(8,128)(2,1)}), bf16[1024,1024]{1,0:T(8,128)(2,1)}) %all-gather.15.cloned.1.call-update) | async-done | bytes 2097168 | tf_op jit(solution)/shard_map/all_gather | solution.py:150
  282.8 17.5 %while.40 = (s32[]{:T(128)}, f32[128,8,2,128]{0,3,2,1:T(8,128)}, bf16[2,512,8,128]{3,2,1,0:T(8,128)(2,1)}, s32[2,512]{1,0:T(2,128)S(1)}, s32[128]{0:T(128)S(1)},...) while((s32[]{:T(128)}, f32[128,8,2,128]{0,3,2,1:T(8,128)}, ...), condition=%wide.region_8.9_spmd.clone, body=%wide.region_7.8_spmd.clone.sunk | while | flops 541655040 | bytes 9058947 | solution.py:185
  302.4 89.7 %all-gather.19.cloned.1.call-done = bf16[1024,2048]{1,0:T(8,128)(2,1)} async-done(((bf16[256,2048]{1,0:T(8,128)(2,1)}), bf16[1024,2048]{1,0:T(8,128)(2,1)}) %all-gather.19.cloned.1.call-update) | async-done | bytes 4194320 | tf_op jit(solution)/shard_map/all_gather | solution.py:103
  397.0 130.1 %all-gather.23.cloned.1.call-done = bf16[1024,3072]{1,0:T(8,128)(2,1)} async-done(((bf16[256,3072]{1,0:T(8,128)(2,1)}), bf16[1024,3072]{1,0:T(8,128)(2,1)}) %all-gather.23.cloned.1.call-update) | async-done | bytes 6291472 | tf_op jit(solution)/shard_map/all_gather | solution.py:108
  527.1 5.0 fusion.77
  532.2 110.1 %all-gather.21.cloned.1.call-done = bf16[1024,3072]{1,0:T(8,128)(2,1)} async-done(((bf16[256,3072]{1,0:T(8,128)(2,1)}), bf16[1024,3072]{1,0:T(8,128)(2,1)}) %all-gather.21.cloned.1.call-update) | async-done | bytes 6291472 | tf_op jit(solution)/shard_map/all_gather | solution.py:106
  646.3 7.3 multiply_convert_fusion
  655.8 6.4 multiply_reduce_fusion.4
  675.6 19.8 %while.41 = (s32[]{:T(128)}, f32[128,8,2,128]{0,3,2,1:T(8,128)}, bf16[2,512,8,128]{3,1,2,0:T(8,128)(2,1)}, bf16[2,512,8,128]{3,1,2,0:T(8,128)(2,1)}, bf16[2,512,...) while((s32[]{:T(128)}, f32[128,8,2,128]{0,3,2,1:T(8,128)}, ...), condition=%wide.region_12.13_spmd.clone, body=%wide.region_11.12_spmd.clone.sunk | while | flops 1354301440 | bytes 76774256 | solution.py:236
  716.5 6.7 convolution_convert_fusion
  723.2 16.5 %reduce-scatter.6.cloned.1.call-done = bf16[128,1024]{1,0:T(8,128)(2,1)} async-done(((bf16[1024,1024]{1,0:T(8,128)(2,1)}), bf16[128,1024]{1,0:T(8,128)(2,1)}) %reduce-scatter.6.cloned.1.call-update) | async-done | bytes 262160 | tf_op jit(solution)/shard_map/reduce_scatter | solution.py:242
  742.0 42.6 %reduce-scatter.8.cloned.1.call-done = bf16[128,1024]{1,0:T(8,128)(2,1)} async-done(((bf16[1024,1024]{1,0:T(8,128)(2,1)}), bf16[128,1024]{1,0:T(8,128)(2,1)}) %reduce-scatter.8.cloned.1.call-update) | async-done | bytes 262160 | tf_op jit(solution)/shard_map/reduce_scatter | solution.py:248
  785.8 7.1 convolution_convert_fusion.1
  792.9 19.7 %pad_maximum_fusion = bf16[1024,15360]{1,0:T(8,128)(2,1)} fusion(bf16[1024,3072]{1,0:T(8,128)(2,1)S(1)} %bitcast.288, bf16[1024,6144]{1,0:T(8,128)(2,1)} %convolution_convert_fusion, bf16[1024,2048]{1,0:T(8,128)(2,1)} %convolution_convert_fusion.2, bf16[1024,4096]{1,0:T(8,128)(2,1)} %convolution_convert_fusion.1), kind=kLoop, calls=%fused_computation.60 | loop fusion | flops 125829120 | bytes 62914560 | tf_op jit(solution)/shard_map/concatenate | solution.py:281
  812.6 515.5 %reduce-scatter.10.cloned.1.call-done = bf16[256,15360]{1,0:T(8,128)(2,1)} async-done(((bf16[1024,15360]{1,0:T(8,128)(2,1)}), bf16[256,15360]{1,0:T(8,128)(2,1)}) %reduce-scatter.10.cloned.1.call-update) | async-done | bytes 7864336
  1328.2 5.8 fusion.51
  1338.1 43.2 %all-reduce.5 = (f32[1024]{0:T(1024)}, f32[128]{0:T(128)}, f32[128]{0:T(128)}, f32[1024]{0:T(1024)}) all-reduce(f32[1024]{0:T(1024)S(1)} %get-tuple-element.333, f32[128]{0:T(128)S(1)} %get-tuple-element.327, f32[128]{0:T(128)S(1)} %get-tuple-element.331, ...), channel_id=1, replica_groups=mesh['fsdp'=4,'ctx'=8] {'fsdp','ctx'}, use_global_device_ids=true, to_apply=%region_19.20 | all-reduce | flops 2304 | bytes 18432 | tf_op jit(solution)/shard_map/psum | solution.py:287
  1382.3 73.2 %all-reduce.8.cloned.1.call-done = bf16[256,15360]{1,0:T(8,128)(2,1)} async-done(((bf16[256,15360]{1,0:T(8,128)(2,1)}), bf16[256,15360]{1,0:T(8,128)(2,1)}) %all-reduce.8.cloned.1.call-update) | async-done | bytes 7864336 | tf_op jit(solution)/shard_map/psum | solution.py:286
  (256 shorter events, 145.4 us)
Async XLA Ops:
  7.2 53.8 %copy-start = (s32[8,2]{0,1:T(2,128)S(1)}, s32[8,2]{0,1:T(2,128)}, u32[]{:S(2)}) copy-start(s32[8,2]{0,1:T(2,128)} %param.21) | copy-start | bytes 196
  7.2 50.8 %all-gather.9.cloned.1.call-start = ((), (), s32[]{:S(2)}) async-start(), calls=%async_computation.3 | async-start | bytes 2621440 | tf_op jit(solution)/shard_map/all_gather | solution.py:102
  7.9 96.1 %all-gather.13.cloned.1.call-start = ((), (), s32[]{:S(2)}) async-start(), calls=%async_computation.5 | async-start | bytes 2621440 | tf_op jit(solution)/shard_map/all_gather | solution.py:101
  8.7 99.3 %copy-start.5 = (bf16[1,128,1024]{2,1,0:T(8,128)(2,1)S(1)}, bf16[1,128,1024]{2,1,0:T(8,128)(2,1)}, u32[]{:S(2)}) copy-start(bf16[1,128,1024]{2,1,0:T(8,128)(2,1)} %param.20) | copy-start | bytes 786436
  8.7 99.3 %copy-start.38 = (f32[1024]{0:T(1024)S(1)}, f32[1024]{0:T(1024)}, u32[]{:S(2)}) copy-start(f32[1024]{0:T(1024)} %param.22) | copy-start | bytes 12292
  8.7 211.5 %all-gather.17.cloned.1.call-start = ((), (), s32[]{:S(2)}) async-start(), calls=%async_computation.7 | async-start | bytes 5242880 | tf_op jit(solution)/shard_map/all_gather | solution.py:100
  9.4 236.6 %all-gather.11.cloned.1.call-start = ((), (), s32[]{:S(2)}) async-start(), calls=%async_computation.4 | async-start | bytes 2359296 | tf_op jit(solution)/shard_map/all_gather | solution.py:151
  10.6 52.3 %copy-start.42 = (f32[128]{0:T(128)}, f32[128]{0:T(128)S(1)}, u32[]{:S(2)}) copy-start(f32[128]{0:T(128)S(1)} %fusion.67) | copy-start | bytes 1540
  60.9 49.5 %copy-start.40 = (f32[128]{0:T(128)S(1)}, f32[128]{0:T(128)}, u32[]{:S(2)}) copy-start(f32[128]{0:T(128)} %param.27) | copy-start | bytes 1540
  60.9 215.3 %all-gather.15.cloned.1.call-start = ((), (), s32[]{:S(2)}) async-start(), calls=%async_computation.6 | async-start | bytes 2359296 | tf_op jit(solution)/shard_map/all_gather | solution.py:150
  111.5 280.7 %all-gather.19.cloned.1.call-start = ((), (), s32[]{:S(2)}) async-start(), calls=%async_computation.8 | async-start | bytes 5242880 | tf_op jit(solution)/shard_map/all_gather | solution.py:103
  112.1 104.6 %copy-start.33 = (bf16[256,3072]{1,0:T(8,128)(2,1)S(1)}, bf16[256,3072]{1,0:T(8,128)(2,1)}, u32[]{:S(2)}) copy-start(bf16[256,3072]{1,0:T(8,128)(2,1)} %param.31) | copy-start | bytes 4718596
  112.1 415.0 %all-gather.23.cloned.1.call-start = ((), (), s32[]{:S(2)}) async-start(), calls=%async_computation.10 | async-start | bytes 7864320 | tf_op jit(solution)/shard_map/all_gather | solution.py:108
  112.8 529.4 %all-gather.21.cloned.1.call-start = ((), (), s32[]{:S(2)}) async-start(), calls=%async_computation.9 | async-start | bytes 7864320 | tf_op jit(solution)/shard_map/all_gather | solution.py:106
  112.9 103.7 %collective-permute-start = (bf16[256,3072]{1,0:T(8,128)(2,1)}, bf16[256,3072]{1,0:T(8,128)(2,1)}, u32[]{:S(2)}, u32[]{:S(2)}) collective-permute-start(bf16[256,3072]{1,0:T(8,128)(2,1)} %param.31), channel_id=1, source_target_pairs={{0,8},{8,0},{16,24},{24,16},{1,9},{9,1},{17,25},{25,17},{2,10},{10... | collective-permute-start | bytes 4718600 | tf_op jit(solution)/shard_map/ppermute | solution.py:16
  113.6 626.2 %reduce-scatter.6.cloned.1.call-start = ((), (), s32[]{:S(2)}) async-start(), calls=%async_computation.11 | async-start | bytes 2359296 | tf_op jit(solution)/shard_map/reduce_scatter | solution.py:242
  220.2 426.0 %collective-permute-start.1 = (bf16[512,3072]{1,0:T(8,128)(2,1)}, bf16[512,3072]{1,0:T(8,128)(2,1)}, u32[]{:S(2)}, u32[]{:S(2)}) collective-permute-start(bf16[512,3072]{1,0:T(8,128)(2,1)} %maximum_select_fusion.1), channel_id=1, source_target_pairs={{0,16},{8,24},{16,0},{24,8},{1,17},{9,25},{17,1},{25,9},{2,18},{10... | collective-permute-start | bytes 9437192 | tf_op jit(solution)/shard_map/ppermute | solution.py:16
  300.3 95.8 %copy-start.39 = (f32[1024]{0:T(1024)S(1)}, f32[1024]{0:T(1024)}, u32[]{:S(2)}) copy-start(f32[1024]{0:T(1024)} %param.29) | copy-start | bytes 12292
  396.1 259.7 %copy-start.14 = (f32[128,1024]{1,0:T(8,128)}, f32[128,1024]{1,0:T(8,128)S(1)}, u32[]{:S(2)}) copy-start(f32[128,1024]{1,0:T(8,128)S(1)} %get-tuple-element.424) | copy-start | bytes 1572868
  700.3 84.3 %reduce-scatter.8.cloned.1.call-start = ((), (), s32[]{:S(2)}) async-start(), calls=%async_computation.12 | async-start | bytes 2359296 | tf_op jit(solution)/shard_map/reduce_scatter | solution.py:248
  703.9 624.3 %reduce-scatter.10.cloned.1.call-start = ((), (), s32[]{:S(2)}) async-start(), calls=%async_computation.14 | async-start | bytes 39321600
  812.6 515.6 %copy-start.15 = (f32[128,1024]{1,0:T(8,128)S(1)}, f32[128,1024]{1,0:T(8,128)}, u32[]{:S(2)}) copy-start(f32[128,1024]{1,0:T(8,128)} %copy-done.14) | copy-start | bytes 1572868
  812.6 642.9 %all-reduce.8.cloned.1.call-start = ((), (), s32[]{:S(2)}) async-start(), calls=%async_computation.13 | async-start | bytes 15728640 | tf_op jit(solution)/shard_map/psum | solution.py:286
  1335.0 46.3 %copy-start.43 = (f32[128]{0:T(128)S(1)}, f32[128]{0:T(128)}, u32[]{:S(2)}) copy-start(f32[128]{0:T(128)} %copy-done.42) | copy-start | bytes 1540
  (45 other events, 205.2 us)
Sparse Core Ops, SparseCore 0:
  9.6 48.3 all-gather.8
  59.5 44.4 all-gather.12
  105.6 110.8 all-gather.16
  218.9 27.1 all-gather.10
  248.4 27.7 all-gather.14
  277.6 114.5 all-gather.18
  393.7 133.3 all-gather.22
  528.7 113.4 all-gather.20
  700.4 39.3 reduce-scatter.5
  743.5 41.1 reduce-scatter.7
  812.7 515.4 reduce-scatter.9
  1331.3 124.0 all-reduce.7
